TPU v7x, 256 devices: a whole 4x4x8 slice. The times are simulated.
256 devices in a mesh: segment: 2 (over core), rows: 32 (over z, x), dp: 4 (over y).
Axes of the slice: x: 4, y: 4, z: 8, core: 2. Of those that a mesh axis runs over, the one named last changes fastest.
Arguments:
- coarse: bfloat16 [8, 100, 384, 256], P(('segment', 'dp'), None, 'rows'), may hold values from -6 to 6
- target: bfloat16 [8, 64, 384, 256], P(('segment', 'dp'), None, 'rows'), may hold values from -6 to 6
- noise: bfloat16 [8, 32, 64, 64, 144], P(('segment', 'dp'), 'rows'), may hold values from -6 to 6
- regions: int32 [8, 32, 32, 4], P(('segment', 'dp')), may hold values from 0 to 244, as said below
- reg_conv: bfloat16 [128, 900], replicated, may hold values from -0.1875 to 0.1875
- reg_out: bfloat16 [64, 128], replicated, may hold values from -0.5 to 0.5
- conv_one: bfloat16 [128, 1152], replicated, may hold values from -0.1875 to 0.1875
- conv_two: bfloat16 [128, 1152], replicated, may hold values from -0.1875 to 0.1875
- out_proj: bfloat16 [64, 128], replicated, may hold values from -0.5 to 0.5
- step_embed: float32 [32, 128], replicated, may hold values from -3 to 3
Outputs:
- mean_field: bfloat16 [8, 64, 384, 256], P(('segment', 'dp'), None, 'rows')
- owner_loss: float32 [8, 32], P(('segment', 'dp'), 'rows')
- grad_conv_one: float32 [128, 1152], replicated
- grad_conv_two: float32 [128, 1152], replicated
- grad_out_proj: float32 [64, 128], replicated
- grad_embed: float32 [32, 128], replicated
Inputs may be any that keep to these rules, and one draw needn't show every extreme that they name: `regions`: for sample s, strip i and entry k: entry 0 is the patch's row offset within strip i (0 on the last strip), entry 1 its first column, at most 244, entry 2 its owner, entry 3 its noise level below 32. Every owner receives 2 * 32, 32 or 16 patches of a sample; for each owner with 64 there is one with 32 and two with 16. No strip lists more than 2 patches for one owner, and some strip lists exactly 2 for one owner.
All inputs are finite; a program needn't handle non-finite values.
Results may differ from a plain program's by a relative error of at most 0.0048.
Values may be sent and summed in bfloat16 or wider, within the bound.
A program may use at most 192 MiB of HBM per device.

v0:
```python
import math
import jax
import jax.numpy as jnp
from jax import lax
from jax.sharding import PartitionSpec as P

PATCH = 12
TAPS = ((-1, -1), (-1, 0), (-1, 1), (0, -1), (0, 0), (0, 1), (1, -1), (1, 0), (1, 1))


def padded_2(cells, sides, width):
    for axis, dim in sides:
        count = lax.axis_size(axis)
        ends = count - 1
        head = lax.slice_in_dim(cells, 0, width, axis=dim)
        tail = lax.slice_in_dim(cells, cells.shape[dim] - width, cells.shape[dim], axis=dim)
        cells = jnp.concatenate(
            [
                lax.ppermute(tail, axis, [(i, (i + 1) % count) for i in range(ends)]),
                cells,
                lax.ppermute(head, axis, [((i + 1) % count, i) for i in range(ends)]),
            ],
            axis=dim,
        )
    return cells


def shifted_2(block, axis, distance):
    devices = range(lax.axis_size(axis))
    route = [(i - distance, i) for i in devices if i - distance in devices]
    return lax.ppermute(block, axis, route)


def shifted(values, row_step, col_step, stride):
    length = values.shape[-1]
    margin = stride + 1
    widths = [(0, 0)] * (values.ndim - 1) + [(margin, margin)]
    padded = jnp.pad(values, widths)
    offset = margin + row_step * stride + col_step
    moved = lax.slice_in_dim(padded, offset, offset + length, axis=values.ndim - 1)
    column = jnp.arange(length, dtype=jnp.int32) % stride + col_step
    inside = (column >= 0) & (column < stride)
    return jnp.where(inside, moved, jnp.zeros((), moved.dtype))


def columns(values, stride):
    return jnp.concatenate(
        [shifted(values, row_step, col_step, stride) for row_step, col_step in TAPS], axis=-2
    )


def fold(gradients, stride):
    width = gradients.shape[-2] // 9
    result = jnp.zeros(gradients.shape[:-2] + (width, gradients.shape[-1]), jnp.float32)
    for position, (row_step, col_step) in enumerate(TAPS):
        piece = gradients[..., position * width : (position + 1) * width, :]
        result = result + shifted(piece, -row_step, -col_step, stride)
    return result


def noise_levels(level_count):
    steps_f = jnp.arange(level_count, dtype=jnp.float32)
    return 0.1 * jnp.exp(steps_f * (math.log(100.0) / (level_count - 1)))


def silu_slope(values):
    gate = jax.nn.sigmoid(values)
    return gate * (1.0 + values * (1.0 - gate))


def product(form, left, right):
    return jnp.einsum(form, left, right, preferred_element_type=jnp.float32)


def regress(grid_rows, reg_conv, reg_out):
    channels, height, width = grid_rows.shape
    flat = grid_rows.reshape(channels, height * width)
    hidden = product("ok,kp->op", reg_conv, columns(flat, width))
    activated = jax.nn.silu(hidden).astype(jnp.bfloat16)
    mean_flat = product("co,op->cp", reg_out, activated).astype(jnp.bfloat16)
    return mean_flat.reshape(reg_out.shape[0], height, width)


def patch_block(mean_part, target_part, noise_part, step_ids, in_use, weights):
    conv_one, conv_two, out_proj, step_embed = weights
    stride = PATCH
    level_count = step_embed.shape[0]
    sigma_table = noise_levels(level_count)
    step_hot = (step_ids[:, None] == jnp.arange(level_count, dtype=jnp.int32)[None, :]).astype(
        jnp.float32
    )
    sigma = jnp.sum(step_hot * sigma_table[None, :], axis=1)
    sigma_sq = sigma * sigma + 1.0
    scale_in = (1.0 / jnp.sqrt(sigma_sq))[:, None, None]
    scale_skip = (1.0 / sigma_sq)[:, None, None]
    scale_out = (sigma / jnp.sqrt(sigma_sq))[:, None, None]
    weight_loss = sigma_sq / (sigma * sigma)
    mean_float = mean_part.astype(jnp.float32)
    residual = target_part.astype(jnp.float32) - mean_float
    noisy = residual + sigma[:, None, None] * noise_part.astype(jnp.float32)
    inputs = jnp.concatenate([scale_in * noisy, mean_float], axis=1).astype(jnp.bfloat16)
    cols_in = columns(inputs, stride)
    embedded = jnp.sum(step_hot[:, :, None] * step_embed[None, :, :], axis=1)
    pre_one = product("ok,bkp->bop", conv_one, cols_in) + embedded[:, :, None]
    act_one = jax.nn.silu(pre_one).astype(jnp.bfloat16)
    cols_one = columns(act_one, stride)
    pre_two = product("ok,bkp->bop", conv_two, cols_one)
    act_two = jax.nn.silu(pre_two).astype(jnp.bfloat16)
    output = product("co,bop->bcp", out_proj, act_two)
    error = scale_skip * noisy + scale_out * output - residual
    losses = weight_loss * jnp.mean(error * error, axis=(1, 2)) * in_use
    factor = 2.0 * weight_loss * in_use / (error.shape[1] * error.shape[2])
    grad_output = (factor[:, None, None] * scale_out * error).astype(jnp.bfloat16)
    grad_proj = product("bcp,bop->co", grad_output, act_two)
    grad_act_two = product("co,bcp->bop", out_proj, grad_output)
    grad_pre_two = (grad_act_two * silu_slope(pre_two)).astype(jnp.bfloat16)
    grad_two = product("bop,bkp->ok", grad_pre_two, cols_one)
    grad_cols = product("ok,bop->bkp", conv_two, grad_pre_two)
    grad_act_one = fold(grad_cols, stride)
    grad_pre_one = (grad_act_one * silu_slope(pre_one)).astype(jnp.bfloat16)
    grad_one = product("bop,bkp->ok", grad_pre_one, cols_in)
    pixel_sums = jnp.sum(grad_pre_one, axis=2, dtype=jnp.float32)
    grad_table = jnp.sum(step_hot[:, :, None] * pixel_sums[:, None, :], axis=0)
    return (losses, (grad_one, grad_two, grad_proj, grad_table))


def run_blocks(mean_part, target_part, noise_part, step_ids, in_use, weights):
    patch_count = mean_part.shape[0]
    blocks = patch_count // 4

    def regroup(values):
        return values.reshape((blocks, 4) + values.shape[1:])

    def advance(running, group_block):
        losses, gradients = patch_block(
            group_block[0], group_block[1], group_block[2], group_block[3], group_block[4], weights
        )
        summed = (
            running[0] + gradients[0],
            running[1] + gradients[1],
            running[2] + gradients[2],
            running[3] + gradients[3],
        )
        return (summed, losses)

    initial = (
        jnp.zeros(weights[0].shape, jnp.float32),
        jnp.zeros(weights[1].shape, jnp.float32),
        jnp.zeros(weights[2].shape, jnp.float32),
        jnp.zeros(weights[3].shape, jnp.float32),
    )
    stacked = (
        regroup(mean_part),
        regroup(target_part),
        regroup(noise_part),
        regroup(step_ids),
        regroup(in_use),
    )
    gradients, losses = lax.scan(advance, initial, stacked)
    return (losses.reshape(patch_count), gradients)


def owner_tables(region_rows, strips):
    owners = region_rows[:, :, 2]
    owner_hot = (owners[:, :, None] == jnp.arange(strips, dtype=jnp.int32)[None, None, :]).astype(
        jnp.int32
    )
    pair_rank = jnp.sum((jnp.cumsum(owner_hot, axis=1) - owner_hot) * owner_hot, axis=2)
    flat_hot = owner_hot.reshape(-1, strips)
    owner_slot = jnp.sum((jnp.cumsum(flat_hot, axis=0) - flat_hot) * flat_hot, axis=1).reshape(
        owners.shape
    )
    return (owners, pair_rank, owner_slot)


def owned_slots(region_rows, owners, pair_rank, owner_slot, strip_index, capacity, most, height):
    strips = region_rows.shape[0]
    slot_hits = (
        (owners == strip_index)[:, :, None]
        & (owner_slot[:, :, None] == jnp.arange(most, dtype=jnp.int32)[None, None, :])
    ).astype(jnp.int32)
    strip_ids = jnp.arange(strips, dtype=jnp.int32)[:, None]
    recv_index = jnp.sum(slot_hits * (strip_ids * capacity + pair_rank)[:, :, None], axis=(0, 1))
    in_use = jnp.sum(slot_hits, axis=(0, 1)).astype(jnp.float32)
    step_ids = jnp.sum(slot_hits * region_rows[:, :, 3][:, :, None], axis=(0, 1))
    row_at = jnp.sum(
        slot_hits * (strip_ids * height + region_rows[:, :, 0])[:, :, None], axis=(0, 1)
    )
    col_at = jnp.sum(slot_hits * region_rows[:, :, 1][:, :, None], axis=(0, 1))
    return (recv_index, in_use, step_ids, row_at, col_at)


def cut_patches(source_grid, row_at, col_at, height):
    zero_index = jnp.zeros((), jnp.int32)

    def cut(row_start, col_start):
        piece = lax.dynamic_slice(
            source_grid,
            (zero_index, zero_index, row_start, col_start),
            (2, source_grid.shape[1], height, height),
        )
        return piece.reshape(2, source_grid.shape[1], height * height)

    return jax.vmap(cut)(row_at, col_at)


def per_device(
    coarse, target, noise, regions, reg_conv, reg_out, conv_one, conv_two, out_proj, step_embed
):
    strips = lax.axis_size("rows")
    strip_index = lax.axis_index("rows")
    region_rows = regions[0]
    per_strip = region_rows.shape[1]
    capacity = max(2, (2 * per_strip + strips - 1) // strips)
    most = 2 * per_strip
    weights = (conv_one, conv_two, out_proj, step_embed)
    rimmed = padded_2(coarse, (("rows", 2),), 1)
    mean_strip = regress(rimmed[0], reg_conv, reg_out)[:, 1:-1]
    height = mean_strip.shape[1]
    pair_strip = jnp.stack([mean_strip, target[0]])
    owners, pair_rank, owner_slot = owner_tables(region_rows, strips)
    own_regions = lax.dynamic_index_in_dim(region_rows, strip_index, 0, keepdims=False)
    own_pairs = lax.dynamic_index_in_dim(pair_rank, strip_index, 0, keepdims=False)
    slot_noise = noise[0, 0]
    below = shifted_2(pair_strip[:, :, : height - 1], "rows", -1)
    extended = jnp.concatenate([pair_strip, below], axis=2)
    patches = cut_patches(extended, own_regions[:, 0], own_regions[:, 1], height)
    outgoing = jnp.zeros((strips, capacity) + patches.shape[1:], patches.dtype)
    outgoing = outgoing.at[own_regions[:, 2], own_pairs].set(patches)
    received = lax.all_to_all(outgoing, "rows", split_axis=0, concat_axis=0, tiled=True)
    flat_recv = received.reshape((strips * capacity,) + patches.shape[1:])
    recv_index, in_use, step_ids, row_at, col_at = owned_slots(
        region_rows, owners, pair_rank, owner_slot, strip_index, capacity, most, height
    )
    gathered = jnp.take(flat_recv, recv_index, axis=0)
    losses, gradients = run_blocks(
        gathered[:, 0], gathered[:, 1], slot_noise, step_ids, in_use, weights
    )
    owner_total = jnp.sum(losses)
    totals = lax.psum(
        (gradients[0], gradients[1], gradients[2], gradients[3]), ("segment", "rows", "dp")
    )
    return (mean_strip[None], owner_total.reshape(1, 1), totals[0], totals[1], totals[2], totals[3])


def solution(mesh):
    placed = (
        P(("segment", "dp"), None, "rows", None),
        P(("segment", "dp"), None, "rows", None),
        P(("segment", "dp"), "rows", None, None, None),
        P(("segment", "dp"), None, None, None),
        P(),
        P(),
        P(),
        P(),
        P(),
        P(),
    )
    return jax.shard_map(
        per_device,
        mesh=mesh,
        in_specs=placed,
        out_specs=(
            P(("segment", "dp"), None, "rows", None),
            P(("segment", "dp"), "rows"),
            P(),
            P(),
            P(),
            P(),
        ),
        check_vma=False,
    )
```

profile of v0, /device:TPU:8, one launch (start us, length us, event | category | flops | bytes accessed | tf_op | source)
XLA Modules:
  0.0 851.5 jit_solution(5382771631686754666)
XLA Ops:
  8.1 3.4 collective-permute-start
  12.8 3.2 copy.114
  18.2 4.4 slice_select_fusion.1
  22.6 41.7 %concatenate.38 = bf16[900,3584]{1,0:T(8,128)(2,1)} concatenate(bf16[100,3584]{1,0:T(8,128)(2,1)} %get-tuple-element.387, bf16[100,3584]{1,0:T(8,128)(2,1)} %get-tuple-element.390, bf16[100,3584]{1,0:T(8,128)(2,1)} %get-tuple-element.380, bf16[100,3584]{1,0:T(8,128)(2,1)} %get-tuple-element.388, bf16[100,3584]{1,0:T(8,128)(2,1)} %get-tuple-element.391, ...), dimensions={0} | concatenate | bytes 12902400 | tf_op jit(solution)/shard_map/concatenate | solution.py:47
  64.3 5.4 fusion.29
  71.2 3.2 copy.113
  74.4 4.9 pad_maximum_fusion.2
  79.3 4.6 copy.115
  87.4 16.4 %collective-permute-done.2 = bf16[2,64,11,256]{3,1,2,0:T(8,128)(2,1)} collective-permute-done((bf16[2,64,11,256]{3,1,2,0:T(8,128)(2,1)}, bf16[2,64,11,256]{3,1,2,0:T(8,128)(2,1)}, u32[]{:S(2)}, u32[]{:S(2)}) %collective-permute-start.2) | collective-permute-done | bytes 720928 | tf_op jit(solution)/shard_map/ppermute | solution.py:31
  103.8 4.7 copy.116
  108.4 8.1 pad_maximum_fusion.1
  116.5 8.6 %gather_fusion = bf16[32,2,64,12,12]{2,1,4,3,0:T(2,128)(2,1)S(1)} fusion(bf16[2,64,23,256]{1,0,3,2:T(2,128)(2,1)} %pad_maximum_fusion.1, s32[32]{0:T(128)S(1)} %get-tuple-element.398), kind=kCustom, calls=%fused_computation | custom fusion | bytes 2359808 | tf_op jit(solution)/shard_map/vmap()/gather | solution.py:197
  125.2 3.9 copy.117
  131.6 5.7 scatter_fusion
  137.3 15.6 %all-to-all-start = ((bf16[32,2,2,64,144]{4,3,2,1,0:T(8,128)(2,1)}), bf16[32,2,2,64,144]{4,3,2,1,0:T(8,128)(2,1)}, u32[]{:S(2)}, u32[]{:S(2)}) async-start(bf16[32,2,2,64,144]{4,3,2,1,0:T(8,128)(2,1)} %scatter_fusion), calls=%async_computation | async-start | bytes 8388608 | tf_op jit(solution)/shard_map/all_to_all | solution.py:230
  153.4 9.0 %reduce-window.6 = s32[32,8,128]{2,1,0:T(8,128)S(1)} reduce-window(s32[32,8,128]{2,1,0:T(8,128)S(1)} %fusion.38, s32[]{:T(128)} %constant.269.clone.1), window={size=1x1x128 pad=0_0x0_0x127_0}, to_apply=%region_0.1 | reduce-window | flops 4161536 | bytes 262148 | tf_op jit(solution)/shard_map/reduce-window
  164.0 81.0 %all-to-all-done = bf16[32,2,2,64,144]{4,3,2,1,0:T(8,128)(2,1)} async-done(((bf16[32,2,2,64,144]{4,3,2,1,0:T(8,128)(2,1)}), bf16[32,2,2,64,144]{4,3,2,1,0:T(8,128)(2,1)}, u32[]{:S(2)}, u32[]{:S(2)}) %all-to-all-start) | async-done | bytes 2359328 | tf_op jit(solution)/shard_map/all_to_all | solution.py:230
  245.0 5.0 gather_fusion.1
  255.2 328.0 %while.21 = (s32[]{:T(128)}, f32[128,1152]{1,0:T(8,128)}, f32[128,1152]{1,0:T(8,128)}, f32[64,128]{1,0:T(8,128)S(1)}, f32[32,128]{1,0:T(8,128)S(1)}, /*index=5*/...) while((s32[]{:T(128)}, f32[128,1152]{1,0:T(8,128)}, ...), condition=%wide.region_15.16_spmd.clone, body=%wide.region_9.15_spmd.clone.sunk | while | flops 884677568 | bytes 48410204 | solution.py:159
  286.9 2.8 fusion.117
  348.6 2.8 fusion.117
  533.7 2.8 fusion.117
  584.5 74.9 %all-reduce.11 = (f32[64,128]{1,0:T(8,128)}, f32[32,128]{1,0:T(8,128)}) all-reduce(f32[64,128]{1,0:T(8,128)S(1)} %get-tuple-element.201, f32[32,128]{1,0:T(8,128)S(1)} %get-tuple-element.202), channel_id=1, replica_groups=mesh['segment'=2,'rows'=32,'dp'=4] {'segment','rows','dp'}, use_global_device_ids=true, to_apply=%region_19.20 | all-reduce | flops 12288 | bytes 98304 | tf_op jit(solution)/shard_map/psum | solution.py:240
  659.4 181.4 %all-reduce.15.cloned.1.call-done = (f32[128,1152]{1,0:T(8,128)}, f32[128,1152]{1,0:T(8,128)}) async-done(((f32[128,1152]{1,0:T(8,128)}, f32[128,1152]{1,0:T(8,128)}), (f32[128,1152]{1,0:T(8,128)}, f32[128,1152]{1,0:T(8,128)})) %all-reduce.15.cloned.1.call-update) | async-done | bytes 1179664 | tf_op jit(solution)/shard_map/psum | solution.py:240
  (917 shorter events, 339.3 us)
Async XLA Ops:
  7.2 57.2 %copy-start = (bf16[128,900]{0,1:T(8,128)(2,1)S(1)}, bf16[128,900]{0,1:T(8,128)(2,1)}, u32[]{:S(2)}) copy-start(bf16[128,900]{0,1:T(8,128)(2,1)} %param.16) | copy-start | bytes 691204
  7.2 10.4 %copy-start.9 = (bf16[1,100,12,256]{3,1,2,0:T(8,128)(2,1)S(1)}, bf16[1,100,12,256]{3,1,2,0:T(8,128)(2,1)}, u32[]{:S(2)}) copy-start(bf16[1,100,12,256]{3,1,2,0:T(8,128)(2,1)} %param.12) | copy-start | bytes 1843204
  8.1 8.8 %collective-permute-start = (bf16[1,100,1,256]{3,1,2,0:T(8,128)(2,1)S(1)}, bf16[1,100,1,256]{3,1,2,0:T(8,128)(2,1)S(1)}, u32[]{:S(2)}, u32[]{:S(2)}) collective-permute-start(bf16[1,100,1,256]{3,1,2,0:T(8,128)(2,1)S(1)} %get-tuple-element.393), channel_id=1, source_target_pairs={{0,4},{4,8},{8,12},{12,16},{16,20},{20,24},{24,28},{28,32},{32,36}... | collective-permute-start | bytes 153608 | tf_op jit(solution)/shard_map/ppermute | solution.py:19
  11.5 6.0 collective-permute-start.1
  22.6 41.7 %copy-start.12 = (bf16[64,128]{1,0:T(8,128)(2,1)S(1)}, bf16[64,128]{1,0:T(8,128)(2,1)}, u32[]{:S(2)}) copy-start(bf16[64,128]{1,0:T(8,128)(2,1)} %param.17) | copy-start | bytes 49156
  83.9 19.9 %collective-permute-start.2 = (bf16[2,64,11,256]{3,1,2,0:T(8,128)(2,1)}, bf16[2,64,11,256]{3,1,2,0:T(8,128)(2,1)}, u32[]{:S(2)}, u32[]{:S(2)}) collective-permute-start(bf16[2,64,11,256]{3,1,2,0:T(8,128)(2,1)} %copy.115), channel_id=1, source_target_pairs={{4,0},{8,4},{12,8},{16,12},{20,16},{24,20},{28,24},{32,28},{36,32}... | collective-permute-start | bytes 2162696 | tf_op jit(solution)/shard_map/ppermute | solution.py:31
  137.3 107.7 %all-to-all-start = ((bf16[32,2,2,64,144]{4,3,2,1,0:T(8,128)(2,1)}), bf16[32,2,2,64,144]{4,3,2,1,0:T(8,128)(2,1)}, u32[]{:S(2)}, u32[]{:S(2)}) async-start(bf16[32,2,2,64,144]{4,3,2,1,0:T(8,128)(2,1)} %scatter_fusion), calls=%async_computation | async-start | bytes 8388608 | tf_op jit(solution)/shard_map/all_to_all | solution.py:230
  152.9 687.9 %all-reduce.15.cloned.1.call-start = ((), (), s32[]{:S(2)}) async-start(), calls=%async_computation.1 | async-start | bytes 2359296 | tf_op jit(solution)/shard_map/psum | solution.py:240
  262.6 2.9 copy-start.2
  282.1 2.9 copy-start.2
  302.7 2.9 copy-start.2
  323.3 2.9 copy-start.2
  343.8 2.9 copy-start.2
  364.4 2.9 copy-start.2
  385.0 2.9 copy-start.2
  405.5 2.9 copy-start.2
  426.1 2.9 copy-start.2
  446.6 2.9 copy-start.2
  467.2 2.9 copy-start.2
  487.8 2.9 copy-start.2
  508.3 2.9 copy-start.2
  528.9 2.9 copy-start.2
  570.0 2.9 copy-start.2
  583.2 261.5 %copy-start.1 = (bf16[128,900]{0,1:T(8,128)(2,1)S(1)}, bf16[128,900]{0,1:T(8,128)(2,1)}, u32[]{:S(2)}) copy-start(bf16[128,900]{0,1:T(8,128)(2,1)} %param.16) | copy-start | bytes 691204
  (69 other events, 102.8 us)
Sparse Core Ops, SparseCore 0:
  583.3 257.4 all-reduce.14
where the time goes:
time: 859 us; the launch traced here: 851 us
  waiting for transfers between devices  279 us (32%)
  matrix products  190 us (22%)
  local copies, waits for them, and re-layouts  148 us (17%)
  other arithmetic  119 us (14%)
  blocking collectives  74.9 us (9%)
  starting transfers between devices  22 us (3%)
  between operations  14.3 us (2%)
    dot_general x129, matrix products, product(): return jnp.einsum(form, left, right, preferred_element_type=jnp.float32)  190 us
    psum x1, waiting for transfers between devices, per_device(): lax.psum((gradients[0], gradients[1], gradients[2], gradients[3]), ('segm...  181 us
    all_to_all x1, waiting for transfers between devices, per_device(): lax.all_to_all(outgoing, 'rows', split_axis=0, concat_axis=0, tiled=True)  81 us
    psum x1, blocking collectives, per_device(): lax.psum((gradients[0], gradients[1], gradients[2], gradients[3]), ('segm...  74.9 us
    concatenate x1, local copies, waits for them, and re-layouts, columns(): jnp.concatenate([shifted(values, row_step, col_step, stride) for row_step...  41.7 us
    while x256, other arithmetic  34.1 us
    another operation x19, other arithmetic  27.5 us
    dynamic_update_slice x16, local copies, waits for them, and re-layouts, run_blocks(): gradients, losses = lax.scan(advance, initial, stacked)  21.3 us
  transfers between devices with their start and end apart: 5, of which 4 were waited for; matrix products, arithmetic and copies ran while one was open for 2% of the time, Pallas kernels for 0%

commit v1 on v0

--- a/solution.py
+++ b/solution.py
@@ -238,7 +238,8 @@
     )
     owner_total = jnp.sum(losses)
     totals = lax.psum(
-        (gradients[0], gradients[1], gradients[2], gradients[3]), ("segment", "rows", "dp")
+        lax.psum((gradients[0], gradients[1], gradients[2], gradients[3]), ("rows", "dp")),
+        "segment",
     )
     return (mean_strip[None], owner_total.reshape(1, 1), totals[0], totals[1], totals[2], totals[3])
 

time: 859 us -> 1500 us (1.75)
  blocking collectives: 74.9 us -> 683 us
  waiting for transfers between devices: 279 us -> 318 us
    psum x1 -> x2, blocking collectives: 74.9 us -> 683 us  [the longest x1 679 us: per_device(): lax.psum((gradients[0], gradients[1], gradients[2], gradients[3]), ('rows...]
    psum x1 -> x2, waiting for transfers between devices: 181 us -> 220 us  [the longest x1 220 us: per_device(): lax.psum((gradients[0], gradients[1], gradients[2], gradients[3]), ('rows...]
    dynamic_update_slice x16, local copies, waits for them, and re-layouts: 21.3 us -> 0.61 us  [run_blocks(): gradients, losses = lax.scan(advance, initial, stacked)]
  transfers between devices with their start and end apart: 5 -> 6, of which waited for: 4 -> 4; matrix products, arithmetic and copies ran while one was open for 2% -> 1% of each run, Pallas kernels for 0% -> 0%
where the time goes in v1:
time: 1500 us; the launch traced here: 1490 us
  blocking collectives  683 us (46%)
  waiting for transfers between devices  318 us (21%)
  matrix products  190 us (13%)
  local copies, waits for them, and re-layouts  138 us (9%)
  other arithmetic  118 us (8%)
  starting transfers between devices  22 us (1%)
    psum x1, blocking collectives, per_device(): lax.psum((gradients[0], gradients[1], gradients[2], gradients[3]), ('rows...  679 us
    psum x1, waiting for transfers between devices, per_device(): lax.psum((gradients[0], gradients[1], gradients[2], gradients[3]), ('rows...  220 us
    dot_general x129, matrix products, product(): return jnp.einsum(form, left, right, preferred_element_type=jnp.float32)  190 us
    all_to_all x1, waiting for transfers between devices, per_device(): lax.all_to_all(outgoing, 'rows', split_axis=0, concat_axis=0, tiled=True)  81 us
    concatenate x1, local copies, waits for them, and re-layouts, columns(): jnp.concatenate([shifted(values, row_step, col_step, stride) for row_step...  41.7 us
    while x256, other arithmetic  34.1 us
  transfers between devices with their start and end apart: 6, of which 4 were waited for; matrix products, arithmetic and copies ran while one was open for 1% of the time, Pallas kernels for 0%

profile of v1, /device:TPU:8, one launch (start us, length us, event | category | flops | bytes accessed | tf_op | source)
XLA Modules:
  0.0 1487.1 jit_solution(7167613610635365401)
XLA Ops:
  8.1 3.4 collective-permute-start
  12.8 3.2 copy.114
  18.2 4.4 slice_select_fusion.1
  22.6 41.7 %concatenate.38 = bf16[900,3584]{1,0:T(8,128)(2,1)} concatenate(bf16[100,3584]{1,0:T(8,128)(2,1)} %get-tuple-element.391, bf16[100,3584]{1,0:T(8,128)(2,1)} %get-tuple-element.394, bf16[100,3584]{1,0:T(8,128)(2,1)} %get-tuple-element.384, bf16[100,3584]{1,0:T(8,128)(2,1)} %get-tuple-element.392, bf16[100,3584]{1,0:T(8,128)(2,1)} %get-tuple-element.395, ...), dimensions={0} | concatenate | bytes 12902400 | tf_op jit(solution)/shard_map/concatenate | solution.py:47
  64.3 5.4 fusion.29
  71.2 3.2 copy.113
  74.4 4.9 pad_maximum_fusion.2
  79.3 4.6 copy.115
  87.4 16.4 %collective-permute-done.2 = bf16[2,64,11,256]{3,1,2,0:T(8,128)(2,1)} collective-permute-done((bf16[2,64,11,256]{3,1,2,0:T(8,128)(2,1)}, bf16[2,64,11,256]{3,1,2,0:T(8,128)(2,1)}, u32[]{:S(2)}, u32[]{:S(2)}) %collective-permute-start.2) | collective-permute-done | bytes 720928 | tf_op jit(solution)/shard_map/ppermute | solution.py:31
  103.8 4.7 copy.116
  108.4 8.1 pad_maximum_fusion.1
  116.5 8.6 gather_fusion
  125.2 3.9 copy.117
  131.6 5.7 scatter_fusion
  137.3 15.6 %all-to-all-start = ((bf16[32,2,2,64,144]{4,3,2,1,0:T(8,128)(2,1)}), bf16[32,2,2,64,144]{4,3,2,1,0:T(8,128)(2,1)}, u32[]{:S(2)}, u32[]{:S(2)}) async-start(bf16[32,2,2,64,144]{4,3,2,1,0:T(8,128)(2,1)} %scatter_fusion), calls=%async_computation | async-start | bytes 8388608 | tf_op jit(solution)/shard_map/all_to_all | solution.py:230
  153.4 9.0 reduce-window.6
  164.0 81.0 %all-to-all-done = bf16[32,2,2,64,144]{4,3,2,1,0:T(8,128)(2,1)} async-done(((bf16[32,2,2,64,144]{4,3,2,1,0:T(8,128)(2,1)}), bf16[32,2,2,64,144]{4,3,2,1,0:T(8,128)(2,1)}, u32[]{:S(2)}, u32[]{:S(2)}) %all-to-all-start) | async-done | bytes 2359328 | tf_op jit(solution)/shard_map/all_to_all | solution.py:230
  245.0 5.0 gather_fusion.1
  255.2 317.5 %while.21 = (s32[]{:T(128)}, f32[128,1152]{1,0:T(8,128)}, f32[128,1152]{1,0:T(8,128)}, f32[64,128]{1,0:T(8,128)S(1)}, f32[32,128]{1,0:T(8,128)S(1)}, /*index=5*/...) while((s32[]{:T(128)}, f32[128,1152]{1,0:T(8,128)}, ...), condition=%wide.region_15.16_spmd.clone, body=%wide.region_9.15_spmd.clone.sunk | while | flops 884677568 | bytes 48410204 | solution.py:159
  286.3 2.8 fusion.117
  306.2 2.8 fusion.117
  572.7 219.7 %all-reduce.18.cloned.1.call-done = (f32[128,1152]{1,0:T(8,128)}, f32[128,1152]{1,0:T(8,128)}) async-done(((f32[128,1152]{1,0:T(8,128)}, f32[128,1152]{1,0:T(8,128)}), (f32[128,1152]{1,0:T(8,128)}, f32[128,1152]{1,0:T(8,128)})) %all-reduce.18.cloned.1.call-update) | async-done | bytes 1179664 | tf_op jit(solution)/shard_map/psum | solution.py:241
  793.0 679.3 %all-reduce.11 = (f32[64,128]{1,0:T(8,128)S(1)}, f32[32,128]{1,0:T(8,128)S(1)}) all-reduce(f32[64,128]{1,0:T(8,128)S(1)} %get-tuple-element.201, f32[32,128]{1,0:T(8,128)S(1)} %get-tuple-element.202), channel_id=1, replica_groups=mesh['segment'=2,'rows'=32,'dp'=4] {'rows','dp'}, use_global_device_ids=true, to_apply=%region_21.22 | all-reduce | flops 12288 | bytes 98304 | tf_op jit(solution)/shard_map/psum | solution.py:241
  1472.3 4.1 all-reduce.13
  (921 shorter events, 330.9 us)
Async XLA Ops:
  7.2 57.2 %copy-start = (bf16[128,900]{0,1:T(8,128)(2,1)S(1)}, bf16[128,900]{0,1:T(8,128)(2,1)}, u32[]{:S(2)}) copy-start(bf16[128,900]{0,1:T(8,128)(2,1)} %param.16) | copy-start | bytes 691204
  7.2 10.4 copy-start.9
  8.1 8.8 collective-permute-start
  11.5 6.0 collective-permute-start.1
  22.6 41.7 %copy-start.12 = (bf16[64,128]{1,0:T(8,128)(2,1)S(1)}, bf16[64,128]{1,0:T(8,128)(2,1)}, u32[]{:S(2)}) copy-start(bf16[64,128]{1,0:T(8,128)(2,1)} %param.17) | copy-start | bytes 49156
  83.9 19.9 %collective-permute-start.2 = (bf16[2,64,11,256]{3,1,2,0:T(8,128)(2,1)}, bf16[2,64,11,256]{3,1,2,0:T(8,128)(2,1)}, u32[]{:S(2)}, u32[]{:S(2)}) collective-permute-start(bf16[2,64,11,256]{3,1,2,0:T(8,128)(2,1)} %copy.115), channel_id=1, source_target_pairs={{4,0},{8,4},{12,8},{16,12},{20,16},{24,20},{28,24},{32,28},{36,32}... | collective-permute-start | bytes 2162696 | tf_op jit(solution)/shard_map/ppermute | solution.py:31
  137.3 107.7 %all-to-all-start = ((bf16[32,2,2,64,144]{4,3,2,1,0:T(8,128)(2,1)}), bf16[32,2,2,64,144]{4,3,2,1,0:T(8,128)(2,1)}, u32[]{:S(2)}, u32[]{:S(2)}) async-start(bf16[32,2,2,64,144]{4,3,2,1,0:T(8,128)(2,1)} %scatter_fusion), calls=%async_computation | async-start | bytes 8388608 | tf_op jit(solution)/shard_map/all_to_all | solution.py:230
  152.9 639.5 %all-reduce.18.cloned.1.call-start = ((), (), s32[]{:S(2)}) async-start(), calls=%async_computation.1 | async-start | bytes 2359296 | tf_op jit(solution)/shard_map/psum | solution.py:241
  262.6 2.9 copy-start.2
  281.5 2.9 copy-start.2
  301.4 2.9 copy-start.2
  321.3 2.9 copy-start.2
  341.2 2.9 copy-start.2
  361.1 2.9 copy-start.2
  381.0 2.9 copy-start.2
  400.9 2.9 copy-start.2
  420.8 2.9 copy-start.2
  440.7 2.9 copy-start.2
  460.7 2.9 copy-start.2
  480.6 2.9 copy-start.2
  500.5 2.9 copy-start.2
  540.3 2.9 copy-start.2
  572.6 907.6 %copy-start.1 = (bf16[128,900]{0,1:T(8,128)(2,1)S(1)}, bf16[128,900]{0,1:T(8,128)(2,1)}, u32[]{:S(2)}) copy-start(bf16[128,900]{0,1:T(8,128)(2,1)} %param.16) | copy-start | bytes 691204
  572.7 903.7 %all-reduce.20.cloned.1.call-start = ((), (), s32[]{:S(2)}) async-start(), calls=%async_computation.2 | async-start | bytes 2359296 | tf_op jit(solution)/shard_map/psum | solution.py:240
  (70 other events, 95.3 us)
Sparse Core Ops, SparseCore 0:
  572.8 219.5 all-reduce.17
  795.0 27.9 all-reduce.19
